TPU v7x, 256 devices: a whole 4x4x8 slice. The times are simulated.
256 devices in a mesh: cls: 2 (over y_hi), dom: 16 (over y_lo, x, core), orient: 8 (over z).
Axes of the slice: x: 4, y: 4 (y_hi: 2, y_lo: 2; y = y_hi * 2 + y_lo), z: 8, core: 2. Of those that a mesh axis runs over, the one named last changes fastest.
Arguments:
- references: bfloat16 [2, 8, 8, 32768], P(None, 'cls', None, ('dom', 'orient')), may hold values from -2 to 2
- images: bfloat16 [2, 2048, 32768], P(None, ('dom', 'orient')), may hold values from -16 to 16
- orient_lists: int32 [2048, 1], P(('dom', 'orient')), may hold values from 0 to 7; in each aligned block of 16 rows (0 to 15, 16 to 31, ...) at most 3 rows name the same one
- shift_ids: int32 [2048, 1], P(('dom', 'orient')), may hold values from 0 to 63
- fixed_weights: float32 [2048, 1], P(('dom', 'orient')), may hold values from 0.2 to 2
Outputs:
- class_prob: float32 [2048, 8], P(('dom', 'orient'), 'cls')
- volume: float32 [2, 8, 8, 32768], P(None, 'cls', 'orient', 'dom')
Inputs may be any that keep to these rules, and one draw needn't show every extreme that they name: `orient_lists`: within the rows of one device (16 particles), no orientation bin is listed by more than 3 particles, a bound that some block reaches.
All inputs are finite; a program needn't handle non-finite values.
Results may differ from a plain program's by a relative error of at most 0.02.
Values may be sent and summed in bfloat16 or wider, within the bound.
A program may use at most 320 MiB of HBM per device.

v0:
```python
import math
import jax
import jax.numpy as jnp
from jax import lax
from jax.sharding import PartitionSpec as P

IMG = 256
TX = 8
TY = 8
TWO_PI = 2.0 * math.pi


def offsets(number):
    return (jnp.arange(number, dtype=jnp.int32) - number // 2).astype(jnp.float32)


def local(references, images, orient_lists, shift_ids, fixed_weights):
    here = images.shape[1]
    classes, orients = (references.shape[1], references.shape[2])
    doms = lax.axis_size("dom")
    band = images.shape[2] // doms
    particles = here * doms
    held = lax.all_to_all(images, "dom", split_axis=2, concat_axis=1, tiled=True)
    piece = lax.all_gather(references, "orient", axis=3, tiled=True)
    ids = lax.all_gather(
        jnp.concatenate([orient_lists, shift_ids], axis=1), "dom", axis=0, tiled=True
    )
    orient_ids, shift_index = (ids[:, 0], ids[:, 1])
    columns = jnp.arange(band, dtype=jnp.int32) + lax.axis_index("dom") * band
    freq_x = (columns % IMG - IMG // 2).astype(jnp.float32)
    freq_y = (columns // IMG).astype(jnp.float32)
    angle_x = TWO_PI / IMG * (offsets(TX)[:, None] * freq_x[None, :])
    angle_y = TWO_PI / IMG * (offsets(TY)[:, None] * freq_y[None, :])
    cx, sx, cy, sy = (jnp.cos(angle_x), jnp.sin(angle_x), jnp.cos(angle_y), jnp.sin(angle_y))
    re, im = (held[0].astype(jnp.float32), held[1].astype(jnp.float32))
    x_re = (re[:, None] * cx - im[:, None] * sx).astype(jnp.bfloat16).reshape(particles * TX, band)
    x_im = (re[:, None] * sx + im[:, None] * cx).astype(jnp.bfloat16).reshape(particles * TX, band)
    r_re = piece[0].reshape(classes * orients, band).astype(jnp.float32)
    r_im = piece[1].reshape(classes * orients, band).astype(jnp.float32)
    s_re = (r_re[None] * cy[:, None] + r_im[None] * sy[:, None]).astype(jnp.bfloat16)
    s_im = (r_im[None] * cy[:, None] - r_re[None] * sy[:, None]).astype(jnp.bfloat16)
    s_re = s_re.reshape(TY * classes * orients, band)
    s_im = s_im.reshape(TY * classes * orients, band)
    part = jnp.einsum("aj,bj->ab", x_re, s_re, preferred_element_type=jnp.float32)
    part = part + jnp.einsum("aj,bj->ab", x_im, s_im, preferred_element_type=jnp.float32)
    part = lax.all_to_all(
        part.reshape(doms, here * TX, -1), "dom", split_axis=0, concat_axis=0, tiled=True
    )
    logits = jnp.sum(part, axis=0).reshape(here, TX, TY, classes, orients)
    top = jnp.max(logits, axis=(1, 2, 3, 4))
    top = lax.pmax(top, "cls")
    exponent = jnp.exp(logits - top[:, None, None, None, None])
    sums = jnp.sum(exponent, axis=(1, 2, 4))
    totals = lax.psum(jnp.sum(sums, axis=1), "cls")
    class_prob = sums / totals[:, None]
    weight = (fixed_weights * class_prob).astype(jnp.bfloat16)
    weight = lax.all_gather(weight, "dom", axis=0, tiled=True)
    entry_x = (shift_index % TX - TX // 2).astype(jnp.float32)
    entry_y = (shift_index // TX - TY // 2).astype(jnp.float32)
    angle = TWO_PI / IMG * (entry_x[:, None] * freq_x[None] + entry_y[:, None] * freq_y[None])
    cosine, sine = (jnp.cos(angle), jnp.sin(angle))
    row_re = (re * cosine - im * sine).astype(jnp.bfloat16)
    row_im = (re * sine + im * cosine).astype(jnp.bfloat16)
    onehot = (orient_ids[:, None] == jnp.arange(orients, dtype=jnp.int32)[None]).astype(
        jnp.bfloat16
    )
    mixing = (onehot[:, :, None] * weight[:, None, :]).reshape(particles, orients * classes)
    grown = [
        jnp.einsum("pm,pj->mj", mixing, row, preferred_element_type=jnp.float32).reshape(
            orients, 1, classes, band
        )
        for row in (row_re, row_im)
    ]
    grown = jnp.concatenate(grown, axis=1)
    grown = lax.all_to_all(grown, "orient", split_axis=0, concat_axis=0, tiled=True)
    volume = jnp.sum(grown, axis=0)[:, :, None, :]
    return (class_prob, volume)


def solution(mesh):
    in_specs = (
        P(None, "cls", None, ("dom", "orient")),
        P(None, ("dom", "orient"), None),
        P(("dom", "orient"), None),
        P(("dom", "orient"), None),
        P(("dom", "orient"), None),
    )
    out_specs = (P(("dom", "orient"), "cls"), P(None, "cls", "orient", "dom"))
    return jax.shard_map(local, mesh=mesh, in_specs=in_specs, out_specs=out_specs, check_vma=False)
```

profile of v0, /device:TPU:1, one launch (start us, length us, event | category | flops | bytes accessed | tf_op | source)
XLA Modules:
  0.0 253.7 jit_solution(4576734842398924274)
XLA Ops:
  0.6 30.9 %copy.31 = bf16[2,16,32768]{1,0,2:T(2,128)(2,1)} copy(bf16[2,16,32768]{2,1,0:T(8,128)(2,1)} %param.6) | data formatting | bytes 4194304 | tf_op args[1]
  31.5 20.8 %reshape.408 = bf16[16,2,32768]{2,1,0:T(2,128)(2,1)} reshape(bf16[32768,2,16]{2,1,0:T(2,128)(2,1)} %bitcast.57) | data formatting | bytes 4194304
  52.3 0.0 copy-start.1
  52.3 7.0 %all-to-all-start = ((bf16[16,2,32768]{2,1,0:T(2,128)(2,1)}), bf16[16,2,32768]{2,1,0:T(2,128)(2,1)S(1)}, u32[]{:S(2)}, u32[]{:S(2)}) async-start(bf16[16,2,32768]{2,1,0:T(2,128)(2,1)} %reshape.408), calls=%async_computation | async-start | bytes 4194304 | tf_op jit(solution)/shard_map/all_to_all | solution.py:23
  59.3 0.0 copy-done.1
  59.3 24.1 %all_gather.9 = bf16[2,4,8,2048]{3,2,1,0:T(8,128)(2,1)S(1)} all-gather(bf16[2,4,8,256]{3,2,1,0:T(8,128)(2,1)S(1)} %copy-done.1), channel_id=1, replica_groups=mesh['cls'=2,'dom'=16,'orient'=8] {'orient'}, dimensions={3}, use_global_device_ids=true | all-gather | bytes 294912 | tf_op jit(solution)/shard_map/all_gather | solution.py:24
  83.5 0.5 fusion.24
  84.0 1.5 subtract_convert_fusion.2
  85.6 1.3 all-to-all-done
  86.9 14.4 %reshape.409 = bf16[32768,2,16]{2,1,0:T(2,128)(2,1)} reshape(bf16[16,2,32768]{2,1,0:T(2,128)(2,1)S(1)} %all-to-all-done) | data formatting | bytes 4194304
  101.3 23.3 %copy.45 = bf16[2,16,16,2048]{3,2,1,0:T(8,128)(2,1)S(1)} copy(bf16[2,16,16,2048]{1,0,3,2:T(2,128)(2,1)} %bitcast.56) | data formatting | bytes 4194304 | tf_op jit(solution)/shard_map/all_to_all | solution.py:23
  124.6 0.5 slice_convert_fusion.1
  125.2 1.2 copy.33
  126.4 0.0 copy-start
  126.4 1.2 copy.34
  127.6 0.0 copy-done
  127.6 2.8 %fusion.1 = f32[2048,256]{1,0:T(8,128)S(1)} fusion(bf16[256,2048]{1,0:T(8,128)(2,1)S(1)} %bitcast.68, f32[8,2048]{1,0:T(8,128)S(1)} %get-tuple-element.15, f32[256,2048]{1,0:T(8,128)S(1)} %bitcast.65, f32[8,2048]{1,0:T(8,128)S(1)} %get-tuple-element.14, f32[256,2048]{1,0:T(8,128)S(1)} %bitcast.63), kind=kOutput, calls=%fused_computation.3 | convolution fusion | flops 2164260864 | bytes 7471104 | tf_op jit(solution)/shard_map/aj,bj->ab/dot_general | solution.py:44
  130.4 3.9 %fusion.14 = f32[2048,256]{1,0:T(8,128)} fusion(f32[2048,256]{1,0:T(8,128)S(1)} %fusion.1, bf16[256,2048]{1,0:T(8,128)(2,1)S(1)} %bitcast.67, f32[8,2048]{1,0:T(8,128)S(1)} %get-tuple-element.15, f32[256,2048]{1,0:T(8,128)S(1)} %bitcast.66, f32[8,2048]{1,0:T(8,128)S(1)} %get-tuple-element.14, f32[256,2048]{1,0:T(8,128)S(1)} %bitcast.64), kind=kOutput, calls=%fused_computation.14 | convolution fusion | flops 2164785152 | bytes 9568256 | tf_op jit(solution)/shard_map/aj,bj->ab/dot_general | solution.py:45
  134.3 0.0 copy-start.3
  134.3 0.0 copy-start.4
  134.3 8.8 %all-to-all-start.1 = ((f32[16,128,256]{2,1,0:T(8,128)}), f32[16,128,256]{2,1,0:T(8,128)}, u32[]{:S(2)}, u32[]{:S(2)}) async-start(f32[16,128,256]{2,1,0:T(8,128)} %bitcast.62), calls=%async_computation.1 | async-start | bytes 4194304 | tf_op jit(solution)/shard_map/all_to_all | solution.py:46
  143.1 0.0 copy-done.3
  143.1 0.0 copy-done.4
  143.1 40.1 %all-gather = s32[16,16,2]{1,2,0:T(2,128)S(1)} all-gather(s32[1,16,2]{1,2,0:T(2,128)S(1)} %add_bitcast_fusion), channel_id=1, replica_groups=mesh['cls'=2,'dom'=16,'orient'=8] {'dom'}, dimensions={0}, use_global_device_ids=true | all-gather | bytes 2176 | tf_op jit(solution)/shard_map/all_gather | solution.py:25
  183.3 0.1 reshape.391
  183.4 0.1 mul.358
  183.5 0.1 copy.38
  183.5 0.1 mul.362
  183.6 0.1 copy.39
  183.7 8.7 %subtract_convert_fusion.1 = (bf16[1,16,16,2048]{3,1,2,0:T(8,128)(2,1)S(1)}, bf16[1,16,16,2048]{3,1,2,0:T(8,128)(2,1)S(1)}) fusion(f32[2048]{0:T(1024)S(1)} %get-tuple-element.23, f32[16,16]{0,1:T(8,128)S(1)} %copy.39, f32[2048]{0:T(1024)S(1)} %get-tuple-element.22, f32[16,16]{0,1:T(8,128)S(1)} %copy.38, bf16[2,16,16,2048]{3,1,2,0:T(8,128)(2,1)S(1)} %bitcast.59), kind=kLoop, calls=%fused_computation.18 | loop fusion | flops 7340032 | bytes 4212736 | tf_op jit(solution)/shard_map/convert_element_type | solution.py:62
  192.4 0.6 copy.40
  193.0 1.6 copy.42
  194.6 0.0 all-to-all-done.1
  194.6 1.7 reduce_sum.43
  196.3 0.1 copy.35
  196.4 0.1 reduce_max.10
  196.5 0.1 reduce_max.14
  196.6 0.1 reduce_max.18
  196.7 5.3 %pmax.7 = f32[16]{0:T(128)S(1)} all-reduce(f32[16]{0:T(128)S(1)} %reduce_max.18), channel_id=1, replica_groups=mesh['cls'=2,'dom'=16,'orient'=8] {'cls'}, use_global_device_ids=true, to_apply=%region_3.4 | all-reduce | flops 16 | bytes 128 | tf_op jit(solution)/shard_map/pmax | solution.py:51
  202.0 0.1 sub.78
  202.1 0.1 sub.79
  202.2 0.2 exponential_reduce_fusion.1
  202.4 0.1 reduce_sum.46
  202.5 0.1 reduce_sum.47
  202.6 5.3 %psum.7 = f32[16]{0:T(128)S(1)} all-reduce(f32[16]{0:T(128)S(1)} %reduce_sum.47), channel_id=1, replica_groups=mesh['cls'=2,'dom'=16,'orient'=8] {'cls'}, use_global_device_ids=true, to_apply=%region_7.8 | all-reduce | flops 16 | bytes 128 | tf_op jit(solution)/shard_map/psum | solution.py:54
  207.9 0.0 copy-start.2
  207.9 1.1 reshape.384
  209.0 0.5 exponential_reduce_fusion
  209.5 0.0 copy-done.2
  209.5 0.6 fusion.36
  210.1 18.2 %all-gather.1 = bf16[16,16,4]{1,2,0:T(4,128)(2,1)S(1)} all-gather(bf16[1,16,4]{1,2,0:T(4,128)(2,1)S(1)} %get-tuple-element.4), channel_id=1, replica_groups=mesh['cls'=2,'dom'=16,'orient'=8] {'dom'}, dimensions={0}, use_global_device_ids=true | all-gather | bytes 2176 | tf_op jit(solution)/shard_map/all_gather | solution.py:57
  228.4 0.1 reshape.393
  228.6 0.3 convolution_bitcast_fusion.1
  228.8 1.5 convolution_bitcast_fusion
  230.4 0.3 copy.44
  230.7 22.2 %all_to_all.25 = f32[8,2,4,2048]{3,2,1,0:T(4,128)S(1)} all-to-all(f32[8,2,4,2048]{3,2,1,0:T(4,128)S(1)} %copy.44), channel_id=1, replica_groups=mesh['cls'=2,'dom'=16,'orient'=8] {'orient'}, dimensions={0} | all-to-all | bytes 1048576 | tf_op jit(solution)/shard_map/all_to_all | solution.py:75
  253.0 0.1 reduce_sum.48
  253.1 0.7 broadcast_in_dim.2
  (13 shorter events, 0.2 us)
Async XLA Ops:
  52.3 7.0 %copy-start.1 = (bf16[2,4,8,256]{3,2,1,0:T(8,128)(2,1)S(1)}, bf16[2,4,8,256]{3,2,1,0:T(8,128)(2,1)}, u32[]{:S(2)}) copy-start(bf16[2,4,8,256]{3,2,1,0:T(8,128)(2,1)} %param.5) | copy-start | bytes 98308
  52.3 34.6 %all-to-all-start = ((bf16[16,2,32768]{2,1,0:T(2,128)(2,1)}), bf16[16,2,32768]{2,1,0:T(2,128)(2,1)S(1)}, u32[]{:S(2)}, u32[]{:S(2)}) async-start(bf16[16,2,32768]{2,1,0:T(2,128)(2,1)} %reshape.408), calls=%async_computation | async-start | bytes 4194304 | tf_op jit(solution)/shard_map/all_to_all | solution.py:23
  126.4 1.2 copy-start
  134.3 8.8 %copy-start.3 = (s32[16,1]{0,1:T(1,128)S(1)}, s32[16,1]{0,1:T(1,128)}, u32[]{:S(2)}) copy-start(s32[16,1]{0,1:T(1,128)} %param.8) | copy-start | bytes 196
  134.3 8.8 %copy-start.4 = (s32[16,1]{0,1:T(1,128)S(1)}, s32[16,1]{0,1:T(1,128)}, u32[]{:S(2)}) copy-start(s32[16,1]{0,1:T(1,128)} %param.7) | copy-start | bytes 196
  134.3 60.3 %all-to-all-start.1 = ((f32[16,128,256]{2,1,0:T(8,128)}), f32[16,128,256]{2,1,0:T(8,128)}, u32[]{:S(2)}, u32[]{:S(2)}) async-start(f32[16,128,256]{2,1,0:T(8,128)} %bitcast.62), calls=%async_computation.1 | async-start | bytes 4194304 | tf_op jit(solution)/shard_map/all_to_all | solution.py:46
  207.9 1.6 copy-start.2
where the time goes:
time: 258 us; the launch traced here: 254 us
  blocking collectives  115 us (45%)
  local copies, waits for them, and re-layouts  97 us (38%)
  starting transfers between devices  15.7 us (6%)
  other arithmetic  15 us (6%)
  matrix products  8.47 us (3%)
    unnamed x15, local copies, waits for them, and re-layouts  66.2 us
    all_gather x1, blocking collectives, local(): lax.all_gather(jnp.concatenate([orient_lists, shift_ids], axis=1), 'dom',...  40.1 us
    all_gather x1, blocking collectives, local(): piece = lax.all_gather(references, 'orient', axis=3, tiled=True)  24.1 us
    all_to_all x1, local copies, waits for them, and re-layouts, local(): lax.all_to_all(images, 'dom', split_axis=2, concat_axis=1, tiled=True)  23.3 us
    all_to_all x1, blocking collectives, local(): lax.all_to_all(grown, 'orient', split_axis=0, concat_axis=0, tiled=True)  22.2 us
    all_gather x1, blocking collectives, local(): weight = lax.all_gather(weight, 'dom', axis=0, tiled=True)  18.2 us
    all_to_all x1, starting transfers between devices, local(): lax.all_to_all(part.reshape(doms, here * TX, -1), 'dom', split_axis=0, co...  8.77 us
    convert_element_type x1, other arithmetic, local(): row_re = (re * cosine - im * sine).astype(jnp.bfloat16)  8.74 us
  transfers between devices with their start and end apart: 2, of which 1 were waited for; matrix products, arithmetic and copies ran while one was open for 5% of the time, Pallas kernels for 0%

commit v1 on v0

--- a/solution.py
+++ b/solution.py
@@ -20,7 +20,10 @@
     doms = lax.axis_size("dom")
     band = images.shape[2] // doms
     particles = here * doms
-    held = lax.all_to_all(images, "dom", split_axis=2, concat_axis=1, tiled=True)
+    held = jnp.concatenate(
+        lax.all_to_all(jnp.stack(jnp.split(images, lax.axis_size("dom"), axis=2)), "dom", 0, 0),
+        axis=1,
+    )
     piece = lax.all_gather(references, "orient", axis=3, tiled=True)
     ids = lax.all_gather(
         jnp.concatenate([orient_lists, shift_ids], axis=1), "dom", axis=0, tiled=True

time: 258 us -> 187 us (0.72); the launches traced: 254 us -> 186 us
  local copies, waits for them, and re-layouts: 97 us -> 28.6 us
    unnamed x15 -> x27, local copies, waits for them, and re-layouts: 66.2 us -> 24.3 us
    all_to_all x1 -> x0, local copies, waits for them, and re-layouts: 23.3 us -> none  [local(): lax.all_to_all(images, 'dom', split_axis=2, concat_axis=1, tiled=True)]
    convert_element_type x4 -> x0, local copies, waits for them, and re-layouts: 4.57 us -> none  [the longest x2 2.44 us: local(): re, im = (held[0].astype(jnp.float32), held[1].astype(jnp.float32))]
  transfers between devices with their start and end apart: 2 -> 2, of which waited for: 1 -> 1; matrix products, arithmetic and copies ran while one was open for 5% -> 6% of each run, Pallas kernels for 0% -> 0%
where the time goes in v1:
time: 187 us; the launch traced here: 186 us
  blocking collectives  115 us (61%)
  local copies, waits for them, and re-layouts  28.6 us (15%)
  other arithmetic  15.9 us (9%)
  starting transfers between devices  15.7 us (8%)
  matrix products  8.48 us (5%)
    all_gather x1, blocking collectives, local(): lax.all_gather(jnp.concatenate([orient_lists, shift_ids], axis=1), 'dom',...  40.1 us
    unnamed x27, local copies, waits for them, and re-layouts  24.3 us
    all_gather x1, blocking collectives, local(): piece = lax.all_gather(references, 'orient', axis=3, tiled=True)  24.1 us
    all_to_all x1, blocking collectives, local(): lax.all_to_all(grown, 'orient', split_axis=0, concat_axis=0, tiled=True)  22.2 us
    all_gather x1, blocking collectives, local(): weight = lax.all_gather(weight, 'dom', axis=0, tiled=True)  18.2 us
    convert_element_type x1, other arithmetic, local(): row_re = (re * cosine - im * sine).astype(jnp.bfloat16)  9.62 us
    all_to_all x1, starting transfers between devices, local(): lax.all_to_all(part.reshape(doms, here * TX, -1), 'dom', split_axis=0, co...  8.75 us
    all_to_all x1, starting transfers between devices, local(): lax.all_to_all(jnp.stack(jnp.split(images, lax.axis_size('dom'), axis=2))...  6.96 us
  transfers between devices with their start and end apart: 2, of which 1 were waited for; matrix products, arithmetic and copies ran while one was open for 6% of the time, Pallas kernels for 0%

profile of v1, /device:TPU:1, one launch (start us, length us, event | category | flops | bytes accessed | tf_op | source)
XLA Modules:
  0.0 186.2 jit_solution(8441519617908995131)
XLA Ops:
  0.6 1.6 bitcast_dynamic-update-slice_fusion.15
  2.2 1.6 bitcast_dynamic-update-slice_fusion.14
  3.7 1.6 bitcast_dynamic-update-slice_fusion.13
  5.3 1.6 bitcast_dynamic-update-slice_fusion.12
  6.9 1.6 bitcast_dynamic-update-slice_fusion.11
  8.4 1.5 bitcast_dynamic-update-slice_fusion.10
  10.0 1.6 bitcast_dynamic-update-slice_fusion.9
  11.6 1.6 bitcast_dynamic-update-slice_fusion.8
  13.1 1.6 bitcast_dynamic-update-slice_fusion.7
  14.7 1.6 bitcast_dynamic-update-slice_fusion.6
  16.3 1.6 bitcast_dynamic-update-slice_fusion.5
  17.8 1.6 bitcast_dynamic-update-slice_fusion.4
  19.4 1.6 bitcast_dynamic-update-slice_fusion.3
  20.9 1.6 bitcast_dynamic-update-slice_fusion.2
  22.5 1.6 bitcast_dynamic-update-slice_fusion.1
  24.0 1.6 bitcast_dynamic-update-slice_fusion
  25.6 0.0 copy-start.1
  25.6 7.0 %all-to-all-start = ((bf16[16,2,16,2048]{3,2,1,0:T(8,128)(2,1)}), bf16[16,2,16,2048]{3,2,1,0:T(8,128)(2,1)S(1)}, u32[]{:S(2)}, u32[]{:S(2)}) async-start(bf16[16,2,16,2048]{3,2,1,0:T(8,128)(2,1)} %bitcast_dynamic-update-slice_fusion), calls=%async_computation | async-start | bytes 4194304 | tf_op jit(solution)/shard_map/all_to_all | solution.py:24
  32.6 0.0 copy-done.1
  32.6 24.1 %all_gather.9 = bf16[2,4,8,2048]{3,2,1,0:T(8,128)(2,1)S(1)} all-gather(bf16[2,4,8,256]{3,2,1,0:T(8,128)(2,1)S(1)} %copy-done.1), channel_id=1, replica_groups=mesh['cls'=2,'dom'=16,'orient'=8] {'orient'}, dimensions={3}, use_global_device_ids=true | all-gather | bytes 294912 | tf_op jit(solution)/shard_map/all_gather | solution.py:27
  56.8 0.5 fusion.24
  57.3 1.5 subtract_convert_fusion.2
  58.9 1.4 all-to-all-done
  60.2 0.0 copy-start
  60.2 0.5 slice_convert_fusion.1
  60.8 0.7 copy-done
  61.5 2.8 %fusion.1 = f32[2048,256]{1,0:T(8,128)S(1)} fusion(bf16[256,2048]{1,0:T(8,128)(2,1)S(1)} %bitcast.95, f32[8,2048]{1,0:T(8,128)S(1)} %get-tuple-element.15, f32[256,2048]{1,0:T(8,128)S(1)} %bitcast.91, f32[8,2048]{1,0:T(8,128)S(1)} %get-tuple-element.14, f32[256,2048]{1,0:T(8,128)S(1)} %bitcast.89), kind=kOutput, calls=%fused_computation.3 | convolution fusion | flops 2164260864 | bytes 7471104 | tf_op jit(solution)/shard_map/aj,bj->ab/dot_general | solution.py:47
  64.2 3.9 %fusion.14 = f32[2048,256]{1,0:T(8,128)} fusion(f32[2048,256]{1,0:T(8,128)S(1)} %fusion.1, bf16[256,2048]{1,0:T(8,128)(2,1)S(1)} %bitcast.94, f32[8,2048]{1,0:T(8,128)S(1)} %get-tuple-element.15, f32[256,2048]{1,0:T(8,128)S(1)} %bitcast.92, f32[8,2048]{1,0:T(8,128)S(1)} %get-tuple-element.14, f32[256,2048]{1,0:T(8,128)S(1)} %bitcast.90), kind=kOutput, calls=%fused_computation.14 | convolution fusion | flops 2164785152 | bytes 9568256 | tf_op jit(solution)/shard_map/aj,bj->ab/dot_general | solution.py:48
  68.2 0.0 copy-start.3
  68.2 0.0 copy-start.4
  68.2 8.8 %all-to-all-start.1 = ((f32[16,128,256]{2,1,0:T(8,128)}), f32[16,128,256]{2,1,0:T(8,128)}, u32[]{:S(2)}, u32[]{:S(2)}) async-start(f32[16,128,256]{2,1,0:T(8,128)} %bitcast.93), calls=%async_computation.1 | async-start | bytes 4194304 | tf_op jit(solution)/shard_map/all_to_all | solution.py:49
  76.9 0.0 copy-done.3
  76.9 0.0 copy-done.4
  77.0 40.1 %all-gather = s32[16,16,2]{1,2,0:T(2,128)S(1)} all-gather(s32[1,16,2]{1,2,0:T(2,128)S(1)} %add_bitcast_fusion), channel_id=1, replica_groups=mesh['cls'=2,'dom'=16,'orient'=8] {'dom'}, dimensions={0}, use_global_device_ids=true | all-gather | bytes 2176 | tf_op jit(solution)/shard_map/all_gather | solution.py:28
  117.1 0.1 reshape.396
  117.2 0.1 mul.358
  117.3 0.1 mul.362
  117.4 9.6 %subtract_convert_fusion.1 = (bf16[1,16,16,2048]{3,2,0,1:T(8,128)(2,1)S(1)}, bf16[1,16,16,2048]{3,2,0,1:T(8,128)(2,1)}) fusion(f32[2048]{0:T(1024)S(1)} %get-tuple-element.23, f32[16,16]{1,0:T(8,128)S(1)} %mul.362, f32[2048]{0:T(1024)S(1)} %get-tuple-element.22, f32[16,16]{1,0:T(8,128)S(1)} %mul.358, bf16[2,16,16,2048]{3,2,0,1:T(8,128)(2,1)S(1)} %bitcast.86), kind=kLoop, calls=%fused_computation.18 | loop fusion | flops 7340032 | bytes 4212736 | tf_op jit(solution)/shard_map/convert_element_type | solution.py:65
  127.0 0.0 all-to-all-done.1
  127.0 1.7 reduce_sum.43
  128.7 0.1 copy.11
  128.8 0.1 reduce_max.10
  129.0 0.1 reduce_max.14
  129.0 0.1 reduce_max.18
  129.2 5.3 %pmax.7 = f32[16]{0:T(128)S(1)} all-reduce(f32[16]{0:T(128)S(1)} %reduce_max.18), channel_id=1, replica_groups=mesh['cls'=2,'dom'=16,'orient'=8] {'cls'}, use_global_device_ids=true, to_apply=%region_3.4 | all-reduce | flops 16 | bytes 128 | tf_op jit(solution)/shard_map/pmax | solution.py:54
  134.5 0.1 sub.78
  134.5 0.1 sub.79
  134.6 0.2 exponential_reduce_fusion.1
  134.8 0.1 reduce_sum.46
  134.9 0.1 reduce_sum.47
  135.0 5.3 %psum.7 = f32[16]{0:T(128)S(1)} all-reduce(f32[16]{0:T(128)S(1)} %reduce_sum.47), channel_id=1, replica_groups=mesh['cls'=2,'dom'=16,'orient'=8] {'cls'}, use_global_device_ids=true, to_apply=%region_7.8 | all-reduce | flops 16 | bytes 128 | tf_op jit(solution)/shard_map/psum | solution.py:57
  140.3 0.0 copy-start.2
  140.3 1.1 reshape.389
  141.5 0.5 exponential_reduce_fusion
  142.0 0.0 copy-done.2
  142.0 0.6 fusion.36
  142.6 18.2 %all-gather.1 = bf16[16,16,4]{1,2,0:T(4,128)(2,1)S(1)} all-gather(bf16[1,16,4]{1,2,0:T(4,128)(2,1)S(1)} %get-tuple-element.4), channel_id=1, replica_groups=mesh['cls'=2,'dom'=16,'orient'=8] {'dom'}, dimensions={0}, use_global_device_ids=true | all-gather | bytes 2176 | tf_op jit(solution)/shard_map/all_gather | solution.py:60
  160.8 0.1 reshape.398
  161.0 1.5 convolution_bitcast_fusion
  162.5 0.3 convolution_bitcast_fusion.1
  162.8 0.3 copy.16
  163.2 22.2 %all_to_all.15 = f32[8,2,4,2048]{3,2,1,0:T(4,128)S(1)} all-to-all(f32[8,2,4,2048]{3,2,1,0:T(4,128)S(1)} %copy.16), channel_id=1, replica_groups=mesh['cls'=2,'dom'=16,'orient'=8] {'orient'}, dimensions={0} | all-to-all | bytes 1048576 | tf_op jit(solution)/shard_map/all_to_all | solution.py:78
  185.4 0.1 reduce_sum.48
  185.5 0.7 broadcast_in_dim.2
  (13 shorter events, 0.2 us)
Async XLA Ops:
  25.6 7.0 %copy-start.1 = (bf16[2,4,8,256]{3,2,1,0:T(8,128)(2,1)S(1)}, bf16[2,4,8,256]{3,2,1,0:T(8,128)(2,1)}, u32[]{:S(2)}) copy-start(bf16[2,4,8,256]{3,2,1,0:T(8,128)(2,1)} %param.5) | copy-start | bytes 98308
  25.6 34.6 %all-to-all-start = ((bf16[16,2,16,2048]{3,2,1,0:T(8,128)(2,1)}), bf16[16,2,16,2048]{3,2,1,0:T(8,128)(2,1)S(1)}, u32[]{:S(2)}, u32[]{:S(2)}) async-start(bf16[16,2,16,2048]{3,2,1,0:T(8,128)(2,1)} %bitcast_dynamic-update-slice_fusion), calls=%async_computation | async-start | bytes 4194304 | tf_op jit(solution)/shard_map/all_to_all | solution.py:24
  60.2 1.2 copy-start
  68.2 8.8 %copy-start.3 = (s32[16,1]{0,1:T(1,128)S(1)}, s32[16,1]{0,1:T(1,128)}, u32[]{:S(2)}) copy-start(s32[16,1]{0,1:T(1,128)} %param.8) | copy-start | bytes 196
  68.2 8.8 %copy-start.4 = (s32[16,1]{0,1:T(1,128)S(1)}, s32[16,1]{0,1:T(1,128)}, u32[]{:S(2)}) copy-start(s32[16,1]{0,1:T(1,128)} %param.7) | copy-start | bytes 196
  68.2 58.8 %all-to-all-start.1 = ((f32[16,128,256]{2,1,0:T(8,128)}), f32[16,128,256]{2,1,0:T(8,128)}, u32[]{:S(2)}, u32[]{:S(2)}) async-start(f32[16,128,256]{2,1,0:T(8,128)} %bitcast.93), calls=%async_computation.1 | async-start | bytes 4194304 | tf_op jit(solution)/shard_map/all_to_all | solution.py:49
  140.3 1.6 copy-start.2
